TPU v7x, 32 devices: a whole 2x2x4 slice. The times are simulated.
32 devices in a mesh: dp: 4 (over y, x), expert: 8 (over z, core).
Axes of the slice: x: 2, y: 2, z: 4, core: 2. Of those that a mesh axis runs over, the one named last changes fastest.
Arguments:
- item_feats: bfloat16 [8, 2048, 256], P('expert', 'dp'), may hold values from -6 to 6
- expert_ids: int32 [8, 2048, 1], P('expert', 'dp'), may hold values from 0 to 31; in each aligned block of 512 rows (0 to 511, 512 to 1023, ..., all dimensions but the last counted through in order) at most 32 rows name the same one
- weight_in: bfloat16 [32, 256, 1024], P('expert'), may hold values from -0.375 to 0.375
- weight_out: bfloat16 [32, 1024, 256], P('expert'), may hold values from -0.1875 to 0.1875
- queries: bfloat16 [8, 2048, 256], P('expert', 'dp'), may hold values from -150 to 150
- query_weight: float32 [8, 2048], P('expert', 'dp'), may hold values from 0.25 to 2
- positives: int32 [8, 2048], P('expert', 'dp'), may hold values from 0 to 2047
- sample_counts: int32 [8, 2048], P('expert'), may hold values from 1 to 4095
Outputs:
- query_loss: float32 [8, 2048], P('expert', 'dp')
- grad_queries: float32 [8, 2048, 256], P('expert', 'dp')
- grad_items: float32 [8, 2048, 256], P('expert', 'dp')
- grad_weight_in: float32 [256, 32, 1024], P('dp', 'expert')
- grad_weight_out: float32 [1024, 32, 256], P('dp', 'expert')
Inputs may be any that keep to these rules, and one draw needn't show every extreme that they name: `expert_ids`: the 512 items of one device name each expert at most 32 times.
All inputs are finite; a program needn't handle non-finite values.
Results may differ from a plain program's by a relative error of at most 0.023.
The roundings to bfloat16 on the way count: a program that leaves them out, or rounds other values in their place, can miss the bound.
Values may be sent and summed in bfloat16 or wider, within the bound.
No kernel may reach another device: no remote copies, remote signals or barrier semaphores. Data moves between devices by JAX's collectives and lax.ppermute only.
A program may use at most 128 MiB of HBM per device.

v0:
```python
import jax
import jax.numpy as jnp
from jax import lax
from jax.sharding import PartitionSpec as P

CAP = 32
norm_eps = 1e-06


def per_device(
    item_feats, expert_ids, weight_in, weight_out, queries, query_weight, positives, sample_counts
):
    groups = lax.axis_size("expert")
    shards = lax.axis_size("dp")
    local_experts = weight_in.shape[0]
    experts_all = local_experts * groups
    item_rows = item_feats.shape[1]
    feat_width = item_feats.shape[2]
    query_rows = queries.shape[1]
    slots_per = CAP
    features = item_feats[0].astype(jnp.float32)
    routes = expert_ids[0, :, 0]
    inv_rms = lax.rsqrt(jnp.mean(features * features, axis=1, keepdims=True) + norm_eps)
    normed = (features * inv_rms).astype(jnp.bfloat16)
    onehot = (routes[:, None] == jnp.arange(experts_all, dtype=jnp.int32)[None, :]).astype(
        jnp.int32
    )
    before = jnp.cumsum(onehot, axis=0) - onehot
    places = routes * slots_per + jnp.sum(before * onehot, axis=1)

    def scatter_slots(values):
        empty = jnp.zeros((experts_all * slots_per, feat_width), jnp.bfloat16)
        return empty.at[places].set(values).reshape(groups, local_experts, slots_per, feat_width)

    expert_received = lax.all_to_all(
        scatter_slots(normed), "expert", split_axis=0, concat_axis=0, tiled=True
    )
    hidden = jnp.einsum(
        "skcd,kdf->skcf", expert_received, weight_in, preferred_element_type=jnp.float32
    )
    expert_active = jax.nn.gelu(hidden).astype(jnp.bfloat16)
    output = jnp.einsum(
        "skcf,kfd->skcd", expert_active, weight_out, preferred_element_type=jnp.float32
    ).astype(jnp.bfloat16)
    output, received, active, hidden = (output, expert_received, expert_active, hidden)
    returned = lax.all_to_all(output, "expert", split_axis=0, concat_axis=0, tiled=True)
    branch = returned.reshape(experts_all * slots_per, feat_width)[places].astype(jnp.float32)
    reduced_sum = features + branch
    length = jnp.sqrt(jnp.sum(reduced_sum * reduced_sum, axis=1, keepdims=True) + norm_eps)
    unit_vecs = reduced_sum / length
    unit_low = unit_vecs.astype(jnp.bfloat16)
    query_matrix = queries[0]
    weights = query_weight[0]
    targets = positives[0]
    log_counts = jnp.log(sample_counts[0].astype(jnp.float32))
    shard_rows = lax.all_gather(unit_low, "dp", axis=0, tiled=True)
    running = jnp.full((query_rows,), -jnp.inf, jnp.float32)
    totals = jnp.zeros((query_rows,), jnp.float32)
    row_count = shard_rows.shape[0]
    scores = (
        jnp.einsum("qd,kd->qk", query_matrix, shard_rows, preferred_element_type=jnp.float32)
        - log_counts[None, :]
    )
    highest = jnp.max(scores, axis=1)
    totals = totals * jnp.exp(running - highest) + jnp.sum(
        jnp.exp(scores - highest[:, None]), axis=1
    )
    columns = jnp.arange(row_count, dtype=jnp.int32)
    picked = jnp.sum(jnp.where(columns[None, :] == targets[:, None], scores, 0.0), axis=1)
    gathered, highest, totals, picked = (shard_rows, highest, totals, picked)
    log_total = highest + jnp.log(totals)
    query_loss = (log_total - picked)[None, :]
    block_layout = gathered.reshape(shards, item_rows, feat_width)
    counts_view = log_counts.reshape(shards, item_rows)

    def weigh_block(inputs):
        item_tile_rows, block_logs, first_item = inputs
        scores = (
            jnp.einsum(
                "qd,kd->qk", query_matrix, item_tile_rows, preferred_element_type=jnp.float32
            )
            - block_logs[None, :]
        )
        columns = first_item + jnp.arange(item_rows, dtype=jnp.int32)
        target_hit = (columns[None, :] == targets[:, None]).astype(jnp.float32)
        return (weights[:, None] * (jnp.exp(scores - log_total[:, None]) - target_hit)).astype(
            jnp.bfloat16
        )

    mixing_factors = lax.map(
        weigh_block, (block_layout, counts_view, jnp.arange(shards, dtype=jnp.int32) * item_rows)
    )
    grad_queries = jnp.einsum(
        "ira,ias->rs", mixing_factors, block_layout, preferred_element_type=jnp.float32
    )
    all_queries = lax.all_gather(query_matrix, "dp", axis=0, tiled=True)
    all_lse, all_weights, all_targets = (
        lax.all_gather(log_total, "dp", axis=0, tiled=True),
        lax.all_gather(weights, "dp", axis=0, tiled=True),
        lax.all_gather(targets.astype(jnp.float32), "dp", axis=0, tiled=True),
    )
    first_item = lax.axis_index("dp") * item_rows
    own_logs = lax.dynamic_slice_in_dim(log_counts, first_item, item_rows)
    scores = (
        jnp.einsum("qd,kd->qk", all_queries, unit_low, preferred_element_type=jnp.float32)
        - own_logs[None, :]
    )
    columns = first_item + jnp.arange(item_rows, dtype=jnp.int32)
    target_hit = (columns[None, :] == all_targets.astype(jnp.int32)[:, None]).astype(jnp.float32)
    terms = (all_weights[:, None] * (jnp.exp(scores - all_lse[:, None]) - target_hit)).astype(
        jnp.bfloat16
    )
    grad_unit = jnp.einsum("qk,qd->kd", terms, all_queries, preferred_element_type=jnp.float32)
    along = jnp.sum(unit_vecs * grad_unit, axis=1, keepdims=True)
    grad_summed = (grad_unit - unit_vecs * along) / length
    grad_low = grad_summed.astype(jnp.bfloat16)
    grad_in = lax.all_to_all(
        scatter_slots(grad_low), "expert", split_axis=0, concat_axis=0, tiled=True
    )
    grad_active = jnp.einsum(
        "skcd,kfd->skcf", grad_in, weight_out, preferred_element_type=jnp.float32
    )
    grad_hidden = jax.vjp(jax.nn.gelu, hidden)[1](grad_active)[0].astype(jnp.bfloat16)
    grad_normed = jnp.einsum(
        "skcf,kdf->skcd", grad_hidden, weight_in, preferred_element_type=jnp.float32
    ).astype(jnp.bfloat16)
    grad_back = lax.all_to_all(grad_normed, "expert", split_axis=0, concat_axis=0, tiled=True)
    grad_rows = grad_back.reshape(experts_all * slots_per, feat_width)[places].astype(jnp.float32)
    projected = jnp.mean(grad_rows * features, axis=1, keepdims=True)
    grad_items = grad_summed + inv_rms * (grad_rows - features * inv_rms * inv_rms * projected)
    cut_rows = received
    grad_weight_in = lax.psum_scatter(
        jnp.einsum(
            "skcr,skcf->rkf", cut_rows, grad_hidden, preferred_element_type=jnp.float32
        ).astype(jnp.bfloat16),
        "dp",
        scatter_dimension=0,
        tiled=True,
    ).astype(jnp.float32)
    cut_rows = active
    grad_weight_out = lax.psum_scatter(
        jnp.einsum("skcr,skcd->rkd", cut_rows, grad_in, preferred_element_type=jnp.float32).astype(
            jnp.bfloat16
        ),
        "dp",
        scatter_dimension=0,
        tiled=True,
    ).astype(jnp.float32)
    return (query_loss, grad_queries[None], grad_items[None], grad_weight_in, grad_weight_out)


def solution(mesh):
    placed = (
        P("expert", "dp", None),
        P("expert", "dp", None),
        P("expert", None, None),
        P("expert", None, None),
        P("expert", "dp", None),
        P("expert", "dp"),
        P("expert", "dp"),
        P("expert", None),
    )
    return jax.shard_map(
        per_device,
        mesh=mesh,
        in_specs=placed,
        out_specs=(
            P("expert", "dp"),
            P("expert", "dp", None),
            P("expert", "dp", None),
            P("dp", "expert", None),
            P("dp", "expert", None),
        ),
        check_vma=False,
    )
```

profile of v0, /device:TPU:0, one launch (start us, length us, event | category | flops | bytes accessed | tf_op | source)
XLA Modules:
  0.0 273.3 jit_solution(7844112702269613480)
XLA Ops:
  12.3 2.5 scatter_custom_fusion
  14.8 21.5 %all_to_all.20 = bf16[8,4,32,256]{3,2,1,0:T(8,128)(2,1)S(1)} all-to-all(bf16[8,4,32,256]{3,2,1,0:T(8,128)(2,1)S(1)} %bitcast.219), channel_id=1, replica_groups=mesh['dp'=4,'expert'=8] {'expert'}, dimensions={0} | all-to-all | bytes 1048576 | tf_op jit(solution)/shard_map/all_to_all | solution.py:35
  36.3 3.5 %fusion.26 = (bf16[8,4,32,1024]{3,2,0,1:T(8,128)(2,1)S(1)}, f32[4,8,32,1024]{3,2,1,0:T(8,128)}) fusion(bf16[4,256,1024]{2,1,0:T(8,128)(2,1)S(1)} %copy-done, bf16[8,4,32,256]{3,2,1,0:T(8,128)(2,1)S(1)} %all_to_all.20), kind=kOutput, calls=%fused_computation.43 | convolution fusion | flops 546308096 | bytes 8912896 | tf_op jit(solution)/shard_map/skcd,kdf->skcf/dot_general | solution.py:38
  42.0 3.5 %all-to-all-start.1 = ((bf16[8,4,32,256]{3,2,1,0:T(8,128)(2,1)}), bf16[8,4,32,256]{3,2,1,0:T(8,128)(2,1)S(1)}, u32[]{:S(2)}, u32[]{:S(2)}) async-start(bf16[8,4,32,256]{3,2,1,0:T(8,128)(2,1)} %copy.40), calls=%async_computation.1 | async-start | bytes 1048576 | tf_op jit(solution)/shard_map/all_to_all | solution.py:46
  45.5 15.2 %all-to-all-done.1 = bf16[8,4,32,256]{3,2,1,0:T(8,128)(2,1)S(1)} async-done(((bf16[8,4,32,256]{3,2,1,0:T(8,128)(2,1)}), bf16[8,4,32,256]{3,2,1,0:T(8,128)(2,1)S(1)}, u32[]{:S(2)}, u32[]{:S(2)}) %all-to-all-start.1) | async-done | bytes 524320 | tf_op jit(solution)/shard_map/all_to_all | solution.py:46
  64.6 8.1 %all-gather.3 = f32[4,1,512]{2,1,0:T(1,128)S(1)} all-gather(f32[1,1,512]{2,1,0:T(1,128)S(1)} %bitcast.239), channel_id=1, replica_groups=mesh['dp'=4,'expert'=8] {'dp'}, dimensions={0}, use_global_device_ids=true | all-gather | bytes 10240 | tf_op jit(solution)/shard_map/all_gather | solution.py:100
  72.7 8.1 %all-gather = f32[1,2048]{1,0:T(1,128)S(1)} all-gather(f32[1,512]{1,0:T(1,128)S(1)} %copy-done.13), channel_id=2, replica_groups=mesh['dp'=4,'expert'=8] {'dp'}, dimensions={1}, use_global_device_ids=true | all-gather | bytes 10240 | tf_op jit(solution)/shard_map/all_gather | solution.py:99
  80.9 8.4 %all-gather.7.cloned.1.call-done = bf16[2048,256]{0,1:T(8,128)(2,1)} async-done(((bf16[512,256]{0,1:T(8,128)(2,1)}), bf16[2048,256]{0,1:T(8,128)(2,1)}) %all-gather.7.cloned.1.call-update) | async-done | bytes 1048592 | tf_op jit(solution)/shard_map/all_gather | solution.py:56
  92.8 8.2 %all-gather.2 = f32[4,1,512]{2,1,0:T(1,128)S(1)} all-gather(f32[1,1,512]{2,1,0:T(1,128)S(1)} %bitcast.232), channel_id=1, replica_groups=mesh['dp'=4,'expert'=8] {'dp'}, dimensions={0}, use_global_device_ids=true | all-gather | bytes 10240 | tf_op jit(solution)/shard_map/all_gather | solution.py:98
  101.0 16.6 %all-gather.9.cloned.1.call-done = bf16[1,2048,256]{2,1,0:T(8,128)(2,1)} async-done(((bf16[1,512,256]{2,1,0:T(8,128)(2,1)}), bf16[1,2048,256]{2,1,0:T(8,128)(2,1)}) %all-gather.9.cloned.1.call-update) | async-done | bytes 1048592 | tf_op jit(solution)/shard_map/all_gather | solution.py:96
  117.6 3.8 %multiply_reduce_fusion = (f32[512]{0:T(512)S(1)}, f32[512,256]{0,1:T(8,128)S(1)}) fusion(f32[512]{0:T(512)S(1)} %add_sqrt_fusion, bf16[512,256]{0,1:T(8,128)(2,1)S(1)} %copy.41, bf16[1,512,256]{1,2,0:T(8,128)(2,1)S(1)} %copy.36, bf16[1,2048,256]{2,1,0:T(8,128)(2,1)} %all-gather.9.cloned.1.call-done, bf16[512,256]{0,1:T(8,128)(2,1)S(1)} %copy-done.7, ...), kind=kOutput, calls=%fused_computation.80 | convolution fusion | flops 1081867776 | bytes 2392064 | tf_op jit(solution)/shard_map/qk,qd->kd/dot_general | solution.py:113
  121.7 3.1 %scatter_custom_fusion.1 = bf16[1024,256]{1,0:T(8,128)(2,1)} fusion(s32[512]{0:T(512)S(1)} %bitcast.235, bf16[512,256]{1,0:T(8,128)(2,1)S(1)} %copy.44, bf16[]{:T(256)} %constant.12.clone.1), kind=kCustom, calls=%fused_computation.85 | custom fusion | bytes 524290 | tf_op jit(solution)/shard_map/scatter | solution.py:33
  124.8 19.9 %all_to_all.21 = bf16[8,4,32,256]{3,2,1,0:T(8,128)(2,1)S(1)} all-to-all(bf16[8,4,32,256]{3,2,1,0:T(8,128)(2,1)} %bitcast.218), channel_id=1, replica_groups=mesh['dp'=4,'expert'=8] {'expert'}, dimensions={0} | all-to-all | bytes 1048576 | tf_op jit(solution)/shard_map/all_to_all | solution.py:117
  144.8 5.9 %fusion.17 = bf16[8,4,32,1024]{3,2,0,1:T(8,128)(2,1)S(1)} fusion(f32[4,8,32,1024]{3,2,1,0:T(8,128)} %get-tuple-element.91, bf16[4,1024,256]{2,1,0:T(8,128)(2,1)} %param.13, bf16[8,4,32,256]{3,2,1,0:T(8,128)(2,1)S(1)} %all_to_all.21), kind=kOutput, calls=%fused_computation.26 | convolution fusion | flops 557842432 | bytes 8912896 | tf_op jit(solution)/shard_map/skcd,kfd->skcf/dot_general | solution.py:120
  154.3 4.6 %copy.49 = bf16[256,4,1024]{2,1,0:T(4,128)(2,1)} copy(bf16[256,4,1024]{0,2,1:T(8,128)(2,1)} %fusion.35) | data formatting | bytes 4194304 | tf_op jit(solution)/shard_map/convert_element_type | solution.py:135
  159.0 3.9 %fusion.36 = bf16[1024,4,256]{0,2,1:T(8,128)(2,1)} fusion(bf16[8,4,32,256]{3,2,1,0:T(8,128)(2,1)} %copy-done.10, bf16[8,4,32,1024]{3,2,0,1:T(8,128)(2,1)} %copy-done.16), kind=kOutput, calls=%fused_computation.55 | convolution fusion | flops 537919488 | bytes 4718592 | tf_op jit(solution)/shard_map/skcr,skcd->rkd/dot_general | solution.py:142
  165.5 2.4 fusion.45
  168.7 3.7 %all-to-all-start.3 = ((bf16[8,4,32,256]{3,2,1,0:T(8,128)(2,1)}), bf16[8,4,32,256]{3,2,1,0:T(8,128)(2,1)S(1)}, u32[]{:S(2)}, u32[]{:S(2)}) async-start(bf16[8,4,32,256]{3,2,1,0:T(8,128)(2,1)} %copy.46), calls=%async_computation.3 | async-start | bytes 1048576 | tf_op jit(solution)/shard_map/all_to_all | solution.py:127
  172.5 14.0 %while.10 = (s32[]{:T(128)}, bf16[4,512,512]{1,2,0:T(8,128)(2,1)}, f32[1,512]{1,0:T(1,128)S(1)}, bf16[4,512,256]{2,1,0:T(8,128)(2,1)}, bf16[512,256]{1,0:T(8,128...) while((s32[]{:T(128)}, bf16[4,512,512]{1,2,0:T(8,128)(2,1)}, ...), condition=%wide.region_10.11_spmd, body=%wide.region_9.10_spmd.sunk | while | flops 136053248 | bytes 1066105 | solution.py:90
  173.7 2.2 fusion.97
  177.2 2.2 fusion.97
  187.1 3.4 %convolution_bitcast_fusion = f32[1,512,256]{2,1,0:T(8,128)} fusion(bf16[4,512,512]{1,2,0:T(8,128)(2,1)} %get-tuple-element.52, bf16[4,512,256]{2,1,0:T(8,128)(2,1)} %get-tuple-element.190), kind=kOutput, calls=%fused_computation.60 | convolution fusion | flops 536870912 | bytes 3670016 | tf_op jit(solution)/shard_map/ira,ias->rs/dot_general | solution.py:93
  196.8 29.7 %all-reduce.3.cloned.1.call-done = bf16[256,4,1024]{2,1,0:T(4,128)(2,1)} async-done(((bf16[256,4,1024]{2,1,0:T(4,128)(2,1)}), bf16[256,4,1024]{2,1,0:T(4,128)(2,1)}) %all-reduce.3.cloned.1.call-update) | async-done | bytes 2097168
  228.6 35.9 %reduce-scatter.2.cloned.1.call-done = bf16[256,4,256]{0,2,1:T(8,128)(2,1)} async-done(((bf16[1024,4,256]{0,2,1:T(8,128)(2,1)}), bf16[256,4,256]{0,2,1:T(8,128)(2,1)}) %reduce-scatter.2.cloned.1.call-update) | async-done | bytes 524304 | tf_op jit(solution)/shard_map/reduce_scatter | solution.py:141
  (105 shorter events, 42.1 us)
Async XLA Ops:
  7.2 29.1 %copy-start = (bf16[4,256,1024]{2,1,0:T(8,128)(2,1)S(1)}, bf16[4,256,1024]{2,1,0:T(8,128)(2,1)}, u32[]{:S(2)}) copy-start(bf16[4,256,1024]{2,1,0:T(8,128)(2,1)} %param.12) | copy-start | bytes 6291460
  36.3 3.5 %copy-start.8 = (bf16[8,4,32,256]{3,2,1,0:T(8,128)(2,1)}, bf16[8,4,32,256]{3,2,1,0:T(8,128)(2,1)S(1)}, u32[]{:S(2)}) copy-start(bf16[8,4,32,256]{3,2,1,0:T(8,128)(2,1)S(1)} %all_to_all.20) | copy-start | bytes 1572868
  36.3 3.5 %copy-start.14 = (bf16[4,1024,256]{2,1,0:T(8,128)(2,1)S(1)}, bf16[4,1024,256]{2,1,0:T(8,128)(2,1)}, u32[]{:S(2)}) copy-start(bf16[4,1024,256]{2,1,0:T(8,128)(2,1)} %param.13) | copy-start | bytes 6291460
  39.8 1.3 copy-start.16
  41.1 23.5 %copy-start.11 = (s32[1,512]{1,0:T(1,128)S(1)}, s32[1,512]{1,0:T(1,128)}, u32[]{:S(2)}) copy-start(s32[1,512]{1,0:T(1,128)} %param.16) | copy-start | bytes 6148
  41.1 31.6 %copy-start.13 = (f32[1,512]{1,0:T(1,128)S(1)}, f32[1,512]{1,0:T(1,128)}, u32[]{:S(2)}) copy-start(f32[1,512]{1,0:T(1,128)} %param.15) | copy-start | bytes 6148
  41.1 39.7 %copy-start.12 = (s32[1,2048]{1,0:T(1,128)S(1)}, s32[1,2048]{1,0:T(1,128)}, u32[]{:S(2)}) copy-start(s32[1,2048]{1,0:T(1,128)} %param.17) | copy-start | bytes 24580
  41.1 48.1 %copy-start.5 = (bf16[1,512,256]{2,1,0:T(8,128)(2,1)S(1)}, bf16[1,512,256]{2,1,0:T(8,128)(2,1)}, u32[]{:S(2)}) copy-start(bf16[1,512,256]{2,1,0:T(8,128)(2,1)} %param.14) | copy-start | bytes 786436
  42.0 18.8 %all-to-all-start.1 = ((bf16[8,4,32,256]{3,2,1,0:T(8,128)(2,1)}), bf16[8,4,32,256]{3,2,1,0:T(8,128)(2,1)S(1)}, u32[]{:S(2)}, u32[]{:S(2)}) async-start(bf16[8,4,32,256]{3,2,1,0:T(8,128)(2,1)} %copy.40), calls=%async_computation.1 | async-start | bytes 1048576 | tf_op jit(solution)/shard_map/all_to_all | solution.py:46
  45.5 43.8 %all-gather.7.cloned.1.call-start = ((), (), s32[]{:S(2)}) async-start(), calls=%async_computation.5 | async-start | bytes 1310720 | tf_op jit(solution)/shard_map/all_gather | solution.py:56
  62.8 58.6 %copy-start.2 = (bf16[512,256]{0,1:T(8,128)(2,1)}, bf16[512,256]{0,1:T(8,128)(2,1)S(1)}, u32[]{:S(2)}) copy-start(bf16[512,256]{0,1:T(8,128)(2,1)S(1)} %copy.41) | copy-start | bytes 786436
  63.8 53.8 %all-gather.9.cloned.1.call-start = ((), (), s32[]{:S(2)}) async-start(), calls=%async_computation.7 | async-start | bytes 1310720 | tf_op jit(solution)/shard_map/all_gather | solution.py:96
  64.5 161.9 %all-reduce.3.cloned.1.call-start = ((), (), s32[]{:S(2)}) async-start(), calls=%async_computation.8 | async-start | bytes 4194304
  91.4 26.2 %copy-start.7 = (bf16[512,256]{0,1:T(8,128)(2,1)S(1)}, bf16[512,256]{0,1:T(8,128)(2,1)}, u32[]{:S(2)}) copy-start(bf16[512,256]{0,1:T(8,128)(2,1)} %fusion.80) | copy-start | bytes 786436
  121.4 29.3 %copy-start.4 = (f32[512,256]{0,1:T(8,128)}, f32[512,256]{0,1:T(8,128)S(1)}, u32[]{:S(2)}) copy-start(f32[512,256]{0,1:T(8,128)S(1)} %get-tuple-element.95) | copy-start | bytes 1572868
  144.8 5.9 %copy-start.10 = (bf16[8,4,32,256]{3,2,1,0:T(8,128)(2,1)}, bf16[8,4,32,256]{3,2,1,0:T(8,128)(2,1)S(1)}, u32[]{:S(2)}) copy-start(bf16[8,4,32,256]{3,2,1,0:T(8,128)(2,1)S(1)} %all_to_all.21) | copy-start | bytes 1572868
  144.8 7.3 %copy-start.9 = (bf16[8,4,32,256]{3,2,1,0:T(8,128)(2,1)S(1)}, bf16[8,4,32,256]{3,2,1,0:T(8,128)(2,1)}, u32[]{:S(2)}) copy-start(bf16[8,4,32,256]{3,2,1,0:T(8,128)(2,1)} %copy-done.8) | copy-start | bytes 1572868
  150.7 1.4 copy-start.17
  158.9 4.1 %copy-start.15 = (u32[32]{0:T(128)S(1)}, u32[32]{0:T(128)}, u32[]{:S(2)}) copy-start(u32[32]{0:T(128)} %constant.70) | copy-start | bytes 388
  158.9 5.3 %copy-start.1 = (bf16[2048,256]{0,1:T(8,128)(2,1)S(1)}, bf16[2048,256]{0,1:T(8,128)(2,1)}, u32[]{:S(2)}) copy-start(bf16[2048,256]{0,1:T(8,128)(2,1)} %all-gather.7.cloned.1.call-done) | copy-start | bytes 3145732
  158.9 105.6 %reduce-scatter.2.cloned.1.call-start = ((), (), s32[]{:S(2)}) async-start(), calls=%async_computation.6 | async-start | bytes 2621440 | tf_op jit(solution)/shard_map/reduce_scatter | solution.py:141
  165.5 6.9 %copy-start.6 = (bf16[1,512,256]{2,1,0:T(8,128)(2,1)S(1)}, bf16[1,512,256]{2,1,0:T(8,128)(2,1)}, u32[]{:S(2)}) copy-start(bf16[1,512,256]{2,1,0:T(8,128)(2,1)} %param.14) | copy-start | bytes 786436
  168.7 21.7 %all-to-all-start.3 = ((bf16[8,4,32,256]{3,2,1,0:T(8,128)(2,1)}), bf16[8,4,32,256]{3,2,1,0:T(8,128)(2,1)S(1)}, u32[]{:S(2)}, u32[]{:S(2)}) async-start(bf16[8,4,32,256]{3,2,1,0:T(8,128)(2,1)} %copy.46), calls=%async_computation.3 | async-start | bytes 1048576 | tf_op jit(solution)/shard_map/all_to_all | solution.py:127
  186.5 6.2 %copy-start.3 = (bf16[512,256]{0,1:T(8,128)(2,1)S(1)}, bf16[512,256]{0,1:T(8,128)(2,1)}, u32[]{:S(2)}) copy-start(bf16[512,256]{0,1:T(8,128)(2,1)} %copy-done.2) | copy-start | bytes 786436
Sparse Core Ops, SparseCore 0:
  63.9 25.3 all-gather.6
  91.1 26.4 all-gather.8
  159.0 67.4 all-reduce.2
  229.3 35.1 reduce-scatter.1
where the time goes:
time: 274 us; the launch traced here: 273 us
  waiting for transfers between devices  106 us (39%)
  blocking collectives  65.8 us (24%)
  matrix products  36.9 us (13%)
  local copies, waits for them, and re-layouts  28.4 us (10%)
  between operations  14.8 us (5%)
  other arithmetic  13.4 us (5%)
  starting transfers between devices  7.37 us (3%)
    reduce_scatter x1, waiting for transfers between devices, per_device(): lax.psum_scatter(jnp.einsum('skcr,skcd->rkd', cut_rows, grad_in, preferre...  35.9 us
    unnamed x5, waiting for transfers between devices  30.4 us
    all_to_all x1, blocking collectives, per_device(): lax.all_to_all(scatter_slots(normed), 'expert', split_axis=0, concat_axis...  21.5 us
    all_to_all x1, blocking collectives, per_device(): lax.all_to_all(scatter_slots(grad_low), 'expert', split_axis=0, concat_ax...  19.9 us
    all_gather x1, waiting for transfers between devices, per_device(): all_queries = lax.all_gather(query_matrix, 'dp', axis=0, tiled=True)  16.6 us
    all_to_all x1, waiting for transfers between devices, per_device(): lax.all_to_all(output, 'expert', split_axis=0, concat_axis=0, tiled=True)  15.2 us
    dot_general x4, matrix products, weigh_block(): jnp.einsum('qd,kd->qk', query_matrix, item_tile_rows, preferred_element_t...  8.95 us
    all_gather x1, waiting for transfers between devices, per_device(): shard_rows = lax.all_gather(unit_low, 'dp', axis=0, tiled=True)  8.37 us
  transfers between devices with their start and end apart: 6, of which 5 were waited for; matrix products, arithmetic and copies ran while one was open for 14% of the time, Pallas kernels for 0%

commit v1 on v0

--- a/solution.py
+++ b/solution.py
@@ -93,7 +93,12 @@
     grad_queries = jnp.einsum(
         "ira,ias->rs", mixing_factors, block_layout, preferred_element_type=jnp.float32
     )
-    all_queries = lax.all_gather(query_matrix, "dp", axis=0, tiled=True)
+    ring = [query_matrix]
+    for hop in range(3):
+        ring.append(lax.ppermute(ring[-1], "dp", [(dev, (dev + 1) % 4) for dev in range(4)]))
+    all_queries = jnp.roll(
+        jnp.concatenate(ring[::-1], axis=0), (lax.axis_index("dp") + 1) * ring[0].shape[0], axis=0
+    )
     all_lse, all_weights, all_targets = (
         lax.all_gather(log_total, "dp", axis=0, tiled=True),
         lax.all_gather(weights, "dp", axis=0, tiled=True),

time: 274 us -> 265 us (0.967)
  waiting for transfers between devices: 106 us -> 81.9 us
  local copies, waits for them, and re-layouts: 28.4 us -> 41 us
    all_gather x1 -> x0, waiting for transfers between devices: 16.6 us -> none  [per_device(): all_queries = lax.all_gather(query_matrix, 'dp', axis=0, tiled=True)]
    ppermute x0 -> x3, waiting for transfers between devices: none -> 16.1 us  [per_device(): lax.ppermute(ring[-1], 'dp', [(dev, (dev + 1) % 4) for dev in range(4)])]
    all_to_all x1, waiting for transfers between devices: 15.2 us -> 0.01 us  [per_device(): lax.all_to_all(output, 'expert', split_axis=0, concat_axis=0, tiled=True)]
    unnamed x40 -> x53, local copies, waits for them, and re-layouts: 8.16 us -> 18.4 us
    all_gather x1, waiting for transfers between devices: 8.37 us -> 1.37 us  [per_device(): shard_rows = lax.all_gather(unit_low, 'dp', axis=0, tiled=True)]
    unnamed x5 -> x4, waiting for transfers between devices: 30.4 us -> 28.4 us
  transfers between devices with their start and end apart: 6 -> 8, of which waited for: 5 -> 5; matrix products, arithmetic and copies ran while one was open for 14% -> 19% of each run, Pallas kernels for 0% -> 0%
where the time goes in v1:
time: 265 us; the launch traced here: 264 us
  waiting for transfers between devices  81.9 us (31%)
  blocking collectives  66.4 us (25%)
  local copies, waits for them, and re-layouts  41 us (15%)
  matrix products  36.5 us (14%)
  between operations  14.8 us (6%)
  other arithmetic  13.6 us (5%)
  starting transfers between devices  9.47 us (4%)
    reduce_scatter x1, waiting for transfers between devices, per_device(): lax.psum_scatter(jnp.einsum('skcr,skcd->rkd', cut_rows, grad_in, preferre...  36 us
    unnamed x4, waiting for transfers between devices  28.4 us
    all_to_all x1, blocking collectives, per_device(): lax.all_to_all(scatter_slots(normed), 'expert', split_axis=0, concat_axis...  21.5 us
    all_to_all x1, blocking collectives, per_device(): lax.all_to_all(scatter_slots(grad_low), 'expert', split_axis=0, concat_ax...  19.9 us
    unnamed x53, local copies, waits for them, and re-layouts  18.4 us
    ppermute x3, waiting for transfers between devices, per_device(): lax.ppermute(ring[-1], 'dp', [(dev, (dev + 1) % 4) for dev in range(4)])  16.1 us
    all_gather x1, blocking collectives, per_device(): lax.all_gather(targets.astype(jnp.float32), 'dp', axis=0, tiled=True)  9.53 us
    dot_general x4, matrix products, weigh_block(): jnp.einsum('qd,kd->qk', query_matrix, item_tile_rows, preferred_element_t...  8.97 us
  transfers between devices with their start and end apart: 8, of which 5 were waited for; matrix products, arithmetic and copies ran while one was open for 19% of the time, Pallas kernels for 0%

profile of v1, /device:TPU:0, one launch (start us, length us, event | category | flops | bytes accessed | tf_op | source)
XLA Modules:
  0.0 263.7 jit_solution(15768600302379769228)
XLA Ops:
  12.3 2.5 scatter_custom_fusion
  14.8 21.5 %all_to_all.20 = bf16[8,4,32,256]{3,2,1,0:T(8,128)(2,1)S(1)} all-to-all(bf16[8,4,32,256]{3,2,1,0:T(8,128)(2,1)S(1)} %bitcast.202), channel_id=1, replica_groups=mesh['dp'=4,'expert'=8] {'expert'}, dimensions={0} | all-to-all | bytes 1048576 | tf_op jit(solution)/shard_map/all_to_all | solution.py:35
  36.3 3.5 %fusion.24 = (bf16[8,4,32,1024]{3,2,0,1:T(8,128)(2,1)S(1)}, f32[4,8,32,1024]{3,2,1,0:T(8,128)}) fusion(bf16[4,256,1024]{2,1,0:T(8,128)(2,1)S(1)} %copy-done, bf16[8,4,32,256]{3,2,1,0:T(8,128)(2,1)S(1)} %all_to_all.20), kind=kOutput, calls=%fused_computation.40 | convolution fusion | flops 546308096 | bytes 8912896 | tf_op jit(solution)/shard_map/skcd,kdf->skcf/dot_general | solution.py:38
  42.0 3.5 %all-to-all-start.1 = ((bf16[8,4,32,256]{3,2,1,0:T(8,128)(2,1)}), bf16[8,4,32,256]{3,2,1,0:T(8,128)(2,1)S(1)}, u32[]{:S(2)}, u32[]{:S(2)}) async-start(bf16[8,4,32,256]{3,2,1,0:T(8,128)(2,1)} %copy.40), calls=%async_computation.1 | async-start | bytes 1048576 | tf_op jit(solution)/shard_map/all_to_all | solution.py:46
  47.1 8.0 %collective-permute-done = bf16[512,256]{1,0:T(8,128)(2,1)S(1)} collective-permute-done((bf16[512,256]{1,0:T(8,128)(2,1)S(1)}, bf16[512,256]{1,0:T(8,128)(2,1)S(1)}, u32[]{:S(2)}, u32[]{:S(2)}) %collective-permute-start) | collective-permute-done | bytes 262176 | tf_op jit(solution)/shard_map/ppermute | solution.py:98
  55.6 8.1 %collective-permute-done.1 = bf16[512,256]{1,0:T(8,128)(2,1)} collective-permute-done((bf16[512,256]{1,0:T(8,128)(2,1)S(1)}, bf16[512,256]{1,0:T(8,128)(2,1)}, u32[]{:S(2)}, u32[]{:S(2)}) %collective-permute-start.1) | collective-permute-done | bytes 262176 | tf_op jit(solution)/shard_map/ppermute | solution.py:98
  63.8 2.6 gather_fusion
  68.6 9.5 %all-gather.2 = f32[4,1,512]{2,1,0:T(1,128)S(1)} all-gather(f32[1,1,512]{2,1,0:T(1,128)S(1)} %bitcast.221), channel_id=1, replica_groups=mesh['dp'=4,'expert'=8] {'dp'}, dimensions={0}, use_global_device_ids=true | all-gather | bytes 10240 | tf_op jit(solution)/shard_map/all_gather | solution.py:105
  78.2 7.2 %all-gather = f32[1,2048]{1,0:T(1,128)S(1)} all-gather(f32[1,512]{1,0:T(1,128)S(1)} %copy-done.16), channel_id=2, replica_groups=mesh['dp'=4,'expert'=8] {'dp'}, dimensions={1}, use_global_device_ids=true | all-gather | bytes 10240 | tf_op jit(solution)/shard_map/all_gather | solution.py:104
  99.9 8.2 %all-gather.1 = f32[4,1,512]{2,1,0:T(1,128)S(1)} all-gather(f32[1,1,512]{2,1,0:T(1,128)S(1)} %bitcast.217), channel_id=1, replica_groups=mesh['dp'=4,'expert'=8] {'dp'}, dimensions={0}, use_global_device_ids=true | all-gather | bytes 10240 | tf_op jit(solution)/shard_map/all_gather | solution.py:103
  108.1 3.6 %multiply_reduce_fusion = (f32[512]{0:T(512)S(1)}, f32[512,256]{0,1:T(8,128)S(1)}) fusion(f32[512]{0:T(512)S(1)} %add_sqrt_fusion, bf16[512,256]{0,1:T(8,128)(2,1)S(1)} %copy.41, bf16[1,512,256]{1,2,0:T(8,128)(2,1)S(1)} %copy.36, bf16[4096,256]{1,0:T(8,128)(2,1)} %constant_dynamic-update-slice_fusion, s32[]{:T(128)S(6)} %select_n.36, ...), kind=kOutput, calls=%fused_computation.77 | convolution fusion | flops 1081867776 | bytes 3441664 | tf_op jit(solution)/shard_map/qk,qd->kd/dot_general | solution.py:118
  112.0 3.1 %scatter_custom_fusion.1 = bf16[1024,256]{1,0:T(8,128)(2,1)} fusion(s32[512]{0:T(512)S(1)} %bitcast.216, bf16[512,256]{1,0:T(8,128)(2,1)S(1)} %copy.44, bf16[]{:T(256)} %constant.33.clone.1), kind=kCustom, calls=%fused_computation.82 | custom fusion | bytes 524290 | tf_op jit(solution)/shard_map/scatter | solution.py:33
  115.2 19.9 %all_to_all.21 = bf16[8,4,32,256]{3,2,1,0:T(8,128)(2,1)S(1)} all-to-all(bf16[8,4,32,256]{3,2,1,0:T(8,128)(2,1)} %bitcast.201), channel_id=1, replica_groups=mesh['dp'=4,'expert'=8] {'expert'}, dimensions={0} | all-to-all | bytes 1048576 | tf_op jit(solution)/shard_map/all_to_all | solution.py:122
  135.1 5.9 %fusion.17 = bf16[8,4,32,1024]{3,2,0,1:T(8,128)(2,1)S(1)} fusion(f32[4,8,32,1024]{3,2,1,0:T(8,128)} %get-tuple-element.91, bf16[4,1024,256]{2,1,0:T(8,128)(2,1)} %param.13, bf16[8,4,32,256]{3,2,1,0:T(8,128)(2,1)S(1)} %all_to_all.21), kind=kOutput, calls=%fused_computation.26 | convolution fusion | flops 557842432 | bytes 8912896 | tf_op jit(solution)/shard_map/skcd,kfd->skcf/dot_general | solution.py:125
  144.6 4.6 %copy.49 = bf16[256,4,1024]{2,1,0:T(4,128)(2,1)} copy(bf16[256,4,1024]{0,2,1:T(8,128)(2,1)} %fusion.33) | data formatting | bytes 4194304 | tf_op jit(solution)/shard_map/convert_element_type | solution.py:140
  150.2 3.7 %fusion.34 = bf16[1024,4,256]{0,2,1:T(8,128)(2,1)} fusion(bf16[8,4,32,256]{3,2,1,0:T(8,128)(2,1)S(1)} %copy-done.13, bf16[8,4,32,1024]{3,2,0,1:T(8,128)(2,1)} %copy-done.19), kind=kOutput, calls=%fused_computation.53 | convolution fusion | flops 537919488 | bytes 4718592 | tf_op jit(solution)/shard_map/skcr,skcd->rkd/dot_general | solution.py:147
  157.2 2.3 fusion.43
  160.3 3.7 %all-to-all-start.3 = ((bf16[8,4,32,256]{3,2,1,0:T(8,128)(2,1)}), bf16[8,4,32,256]{3,2,1,0:T(8,128)(2,1)S(1)}, u32[]{:S(2)}, u32[]{:S(2)}) async-start(bf16[8,4,32,256]{3,2,1,0:T(8,128)(2,1)} %copy.46), calls=%async_computation.3 | async-start | bytes 1048576 | tf_op jit(solution)/shard_map/all_to_all | solution.py:132
  164.1 14.0 %while.10 = (s32[]{:T(128)}, bf16[4,512,512]{1,2,0:T(8,128)(2,1)}, f32[1,512]{1,0:T(1,128)S(1)}, bf16[4,512,256]{2,1,0:T(8,128)(2,1)}, bf16[512,256]{1,0:T(8,128...) while((s32[]{:T(128)}, bf16[4,512,512]{1,2,0:T(8,128)(2,1)}, ...), condition=%wide.region_10.11_spmd, body=%wide.region_9.10_spmd.sunk | while | flops 136053248 | bytes 1066113 | solution.py:90
  168.8 2.2 fusion.95
  172.3 2.3 fusion.95
  178.6 3.4 %convolution_bitcast_fusion = f32[1,512,256]{2,1,0:T(8,128)} fusion(bf16[4,512,512]{1,2,0:T(8,128)(2,1)} %get-tuple-element.52, bf16[4,512,256]{2,1,0:T(8,128)(2,1)} %get-tuple-element.189), kind=kOutput, calls=%fused_computation.58 | convolution fusion | flops 536870912 | bytes 3670016 | tf_op jit(solution)/shard_map/ira,ias->rs/dot_general | solution.py:93
  188.4 28.4 %all-reduce.3.cloned.1.call-done = bf16[256,4,1024]{2,1,0:T(4,128)(2,1)} async-done(((bf16[256,4,1024]{2,1,0:T(4,128)(2,1)}), bf16[256,4,1024]{2,1,0:T(4,128)(2,1)}) %all-reduce.3.cloned.1.call-update) | async-done | bytes 2097168
  218.9 36.0 %reduce-scatter.2.cloned.1.call-done = bf16[256,4,256]{0,2,1:T(8,128)(2,1)} async-done(((bf16[1024,4,256]{0,2,1:T(8,128)(2,1)}), bf16[256,4,256]{0,2,1:T(8,128)(2,1)}) %reduce-scatter.2.cloned.1.call-update) | async-done | bytes 524304 | tf_op jit(solution)/shard_map/reduce_scatter | solution.py:146
  (122 shorter events, 55.1 us)
Async XLA Ops:
  7.2 29.1 %copy-start = (bf16[4,256,1024]{2,1,0:T(8,128)(2,1)S(1)}, bf16[4,256,1024]{2,1,0:T(8,128)(2,1)}, u32[]{:S(2)}) copy-start(bf16[4,256,1024]{2,1,0:T(8,128)(2,1)} %param.12) | copy-start | bytes 6291460
  36.3 3.5 %copy-start.10 = (bf16[8,4,32,256]{3,2,1,0:T(8,128)(2,1)}, bf16[8,4,32,256]{3,2,1,0:T(8,128)(2,1)S(1)}, u32[]{:S(2)}) copy-start(bf16[8,4,32,256]{3,2,1,0:T(8,128)(2,1)S(1)} %all_to_all.20) | copy-start | bytes 1572868
  36.3 3.5 %copy-start.17 = (bf16[4,1024,256]{2,1,0:T(8,128)(2,1)S(1)}, bf16[4,1024,256]{2,1,0:T(8,128)(2,1)}, u32[]{:S(2)}) copy-start(bf16[4,1024,256]{2,1,0:T(8,128)(2,1)} %param.13) | copy-start | bytes 6291460
  41.1 4.4 %copy-start.4 = (bf16[1,512,256]{2,1,0:T(8,128)(2,1)S(1)}, bf16[1,512,256]{2,1,0:T(8,128)(2,1)}, u32[]{:S(2)}) copy-start(bf16[1,512,256]{2,1,0:T(8,128)(2,1)} %param.14) | copy-start | bytes 786436
  42.0 21.8 %all-to-all-start.1 = ((bf16[8,4,32,256]{3,2,1,0:T(8,128)(2,1)}), bf16[8,4,32,256]{3,2,1,0:T(8,128)(2,1)S(1)}, u32[]{:S(2)}, u32[]{:S(2)}) async-start(bf16[8,4,32,256]{3,2,1,0:T(8,128)(2,1)} %copy.40), calls=%async_computation.1 | async-start | bytes 1048576 | tf_op jit(solution)/shard_map/all_to_all | solution.py:46
  45.5 50.9 %all-gather.5.cloned.1.call-start = ((), (), s32[]{:S(2)}) async-start(), calls=%async_computation.5 | async-start | bytes 1310720 | tf_op jit(solution)/shard_map/all_gather | solution.py:56
  45.5 9.5 %collective-permute-start = (bf16[512,256]{1,0:T(8,128)(2,1)S(1)}, bf16[512,256]{1,0:T(8,128)(2,1)S(1)}, u32[]{:S(2)}, u32[]{:S(2)}) collective-permute-start(bf16[512,256]{1,0:T(8,128)(2,1)S(1)} %bitcast.199), channel_id=1, source_target_pairs={{0,8},{8,16},{16,24},{24,0},{1,9},{9,17},{17,25},{25,1},{2,10},{10... | collective-permute-start | bytes 786440 | tf_op jit(solution)/shard_map/ppermute | solution.py:98
  55.0 8.7 %copy-start.8 = (bf16[512,256]{1,0:T(8,128)(2,1)}, bf16[512,256]{1,0:T(8,128)(2,1)S(1)}, u32[]{:S(2)}) copy-start(bf16[512,256]{1,0:T(8,128)(2,1)S(1)} %collective-permute-done) | copy-start | bytes 786436
  55.0 8.7 %collective-permute-start.1 = (bf16[512,256]{1,0:T(8,128)(2,1)S(1)}, bf16[512,256]{1,0:T(8,128)(2,1)}, u32[]{:S(2)}, u32[]{:S(2)}) collective-permute-start(bf16[512,256]{1,0:T(8,128)(2,1)S(1)} %collective-permute-done), channel_id=1, source_target_pairs={{0,8},{8,16},{16,24},{24,0},{1,9},{9,17},{17,25},{25,1},{2,10},{10... | collective-permute-start | bytes 786440 | tf_op jit(solution)/shard_map/ppermute | solution.py:98
  63.8 21.7 %collective-permute-start.2 = (bf16[512,256]{1,0:T(8,128)(2,1)}, bf16[512,256]{1,0:T(8,128)(2,1)}, u32[]{:S(2)}, u32[]{:S(2)}) collective-permute-start(bf16[512,256]{1,0:T(8,128)(2,1)} %collective-permute-done.1), channel_id=1, source_target_pairs={{0,8},{8,16},{16,24},{24,0},{1,9},{9,17},{17,25},{25,1},{2,10},{10... | collective-permute-start | bytes 786440 | tf_op jit(solution)/shard_map/ppermute | solution.py:98
  63.8 4.8 %copy-start.15 = (s32[1,2048]{1,0:T(1,128)S(1)}, s32[1,2048]{1,0:T(1,128)}, u32[]{:S(2)}) copy-start(s32[1,2048]{1,0:T(1,128)} %param.17) | copy-start | bytes 24580
  63.8 4.8 %copy-start.14 = (s32[1,512]{1,0:T(1,128)S(1)}, s32[1,512]{1,0:T(1,128)}, u32[]{:S(2)}) copy-start(s32[1,512]{1,0:T(1,128)} %param.16) | copy-start | bytes 6148
  63.8 14.4 %copy-start.16 = (f32[1,512]{1,0:T(1,128)S(1)}, f32[1,512]{1,0:T(1,128)}, u32[]{:S(2)}) copy-start(f32[1,512]{1,0:T(1,128)} %param.15) | copy-start | bytes 6148
  66.4 22.4 %copy-start.9 = (bf16[512,256]{1,0:T(8,128)(2,1)S(1)}, bf16[512,256]{1,0:T(8,128)(2,1)}, u32[]{:S(2)}) copy-start(bf16[512,256]{1,0:T(8,128)(2,1)} %copy-done.8) | copy-start | bytes 786436
  67.5 44.2 %copy-start.2 = (bf16[512,256]{0,1:T(8,128)(2,1)}, bf16[512,256]{0,1:T(8,128)(2,1)S(1)}, u32[]{:S(2)}) copy-start(bf16[512,256]{0,1:T(8,128)(2,1)S(1)} %copy.41) | copy-start | bytes 786436
  68.5 148.3 %all-reduce.3.cloned.1.call-start = ((), (), s32[]{:S(2)}) async-start(), calls=%async_computation.7 | async-start | bytes 4194304
  98.6 9.6 %copy-start.7 = (bf16[512,256]{0,1:T(8,128)(2,1)S(1)}, bf16[512,256]{0,1:T(8,128)(2,1)}, u32[]{:S(2)}) copy-start(bf16[512,256]{0,1:T(8,128)(2,1)} %fusion.78) | copy-start | bytes 786436
  111.7 29.3 %copy-start.6 = (f32[512,256]{0,1:T(8,128)}, f32[512,256]{0,1:T(8,128)S(1)}, u32[]{:S(2)}) copy-start(f32[512,256]{0,1:T(8,128)S(1)} %get-tuple-element.95) | copy-start | bytes 1572868
  135.1 5.9 %copy-start.12 = (bf16[8,4,32,256]{3,2,1,0:T(8,128)(2,1)}, bf16[8,4,32,256]{3,2,1,0:T(8,128)(2,1)S(1)}, u32[]{:S(2)}) copy-start(bf16[8,4,32,256]{3,2,1,0:T(8,128)(2,1)S(1)} %all_to_all.21) | copy-start | bytes 1572868
  135.1 7.3 %copy-start.11 = (bf16[8,4,32,256]{3,2,1,0:T(8,128)(2,1)S(1)}, bf16[8,4,32,256]{3,2,1,0:T(8,128)(2,1)}, u32[]{:S(2)}) copy-start(bf16[8,4,32,256]{3,2,1,0:T(8,128)(2,1)} %copy-done.10) | copy-start | bytes 1572868
  149.2 105.7 %reduce-scatter.2.cloned.1.call-start = ((), (), s32[]{:S(2)}) async-start(), calls=%async_computation.6 | async-start | bytes 2621440 | tf_op jit(solution)/shard_map/reduce_scatter | solution.py:146
  159.5 4.6 %copy-start.5 = (bf16[1,512,256]{2,1,0:T(8,128)(2,1)S(1)}, bf16[1,512,256]{2,1,0:T(8,128)(2,1)}, u32[]{:S(2)}) copy-start(bf16[1,512,256]{2,1,0:T(8,128)(2,1)} %param.14) | copy-start | bytes 786436
  160.3 21.7 %all-to-all-start.3 = ((bf16[8,4,32,256]{3,2,1,0:T(8,128)(2,1)}), bf16[8,4,32,256]{3,2,1,0:T(8,128)(2,1)S(1)}, u32[]{:S(2)}, u32[]{:S(2)}) async-start(bf16[8,4,32,256]{3,2,1,0:T(8,128)(2,1)} %copy.46), calls=%async_computation.3 | async-start | bytes 1048576 | tf_op jit(solution)/shard_map/all_to_all | solution.py:132
  182.1 2.2 copy-start.3
  (5 other events, 6.3 us)
Sparse Core Ops, SparseCore 0:
  68.6 27.7 all-gather.4
  149.3 67.3 all-reduce.2
  219.7 35.1 reduce-scatter.1
